TPU v7x, 32 devices: a whole 2x2x4 slice. The times are simulated.
32 devices in a mesh: ka: 8 (over z, y), col: 4 (over x, core).
Axes of the slice: x: 2, y: 2, z: 4, core: 2. Of those that a mesh axis runs over, the one named last changes fastest.
Arguments:
- amps: bfloat16 [16, 256, 192], P('ka', 'col'), may hold values from -6 to 6
- isdf_coeffs: bfloat16 [16, 2048, 256], P('ka', 'col'), may hold values from -0.375 to 0.375
- w_screen: bfloat16 [16, 2048, 2048], P(None, 'ka', 'col'), as said below
- energies: float32 [16, 256], P('ka', 'col'), may hold values from 0.5 to 3
- qsel: int32 [2], replicated, may hold values from 0 to 15
- partner: int32 [2, 16], replicated, may hold values from 0 to 15, each once within a row
Outputs:
- applied: float32 [16, 256, 192], P('ka', 'col')
Inputs may be any that keep to these rules, and one draw needn't show every extreme that they name: Each row of partner is a permutation of the 16 k points. `w_screen`: each of the 16 matrices is symmetric.
All inputs are finite; a program needn't handle non-finite values.
Results may differ from a plain program's by a relative error of at most 0.013.
Values may be sent and summed in bfloat16 or wider, within the bound.
A program may use at most 64 MiB of HBM per device.

v0:
```python
import jax
import jax.numpy as jnp
from jax import lax
from jax.sharding import PartitionSpec as P


def body(amps, isdf_coeffs, w_screen, energies, qsel, partner):
    k_local = amps.shape[0]
    vectors = amps.shape[2]
    offset_base = lax.axis_index("ka") * k_local
    owned = offset_base + jnp.arange(k_local, dtype=jnp.int32)
    wanted = jnp.take(partner, owned, axis=1).reshape(-1)
    everyone = lax.all_gather(amps, "ka", axis=0, tiled=True)
    picked = jnp.take(everyone, wanted, axis=0)
    partners = lax.all_gather(picked, "col", axis=1, tiled=True)
    partners = partners.reshape(2, k_local, partners.shape[1], vectors)
    densities = jnp.einsum(
        "kms,qkse->qmke", isdf_coeffs, partners, preferred_element_type=jnp.float32
    )
    width = densities.shape[1]
    densities = densities.astype(jnp.bfloat16).reshape(2, width, k_local * vectors)
    slabs = jnp.take(w_screen, qsel, axis=0)
    partials = jnp.einsum(
        "qrm,qmx->qrx",
        lax.all_gather(slabs, "ka", axis=1, tiled=True),
        densities,
        preferred_element_type=jnp.float32,
    )
    screened = lax.psum_scatter(
        partials.astype(jnp.bfloat16), "col", scatter_dimension=1, tiled=True
    ).astype(jnp.float32)
    screened = screened.astype(jnp.bfloat16).reshape(2, width, k_local, vectors)
    projected = jnp.einsum(
        "kms,qmke->kse", isdf_coeffs, screened, preferred_element_type=jnp.float32
    )
    summed = lax.psum_scatter(
        projected.astype(jnp.bfloat16), "col", scatter_dimension=1, tiled=True
    ).astype(jnp.float32)
    return summed + energies[:, :, None] * amps.astype(jnp.float32)


def solution(mesh):
    placed = (
        P("ka", "col", None),
        P("ka", "col", None),
        P(None, "ka", "col"),
        P("ka", "col"),
        P(),
        P(),
    )
    return jax.shard_map(
        body, mesh=mesh, in_specs=placed, out_specs=P("ka", "col", None), check_vma=False
    )
```

profile of v0, /device:TPU:0, one launch (start us, length us, event | category | flops | bytes accessed | tf_op | source)
XLA Modules:
  0.0 176.6 jit_solution(11480643661953069329)
XLA Ops:
  6.5 0.0 copy-start
  6.5 0.0 all-gather.2.cloned.1.call-start
  6.5 0.7 compare_select_fusion.4
  7.3 0.7 compare_and_fusion.2
  7.9 2.8 %gather_fusion = bf16[2,256,512]{2,1,0:T(8,128)(2,1)S(1)} fusion(bf16[16,256,512]{2,1,0:T(8,128)(2,1)} %param.8, s32[1024]{0:T(1024)S(1)} %pad_clamp_fusion.2), kind=kCustom, calls=%fused_computation | custom fusion | bytes 1048584 | tf_op jit(solution)/shard_map/jit(_take)/gather | solution.py:22
  10.7 0.9 broadcast_select_fusion
  11.6 0.0 all-gather.2.cloned.1.call-update
  11.7 0.0 reduce-scatter.2.cloned.1.call-start
  11.7 0.8 copy.53
  12.5 0.6 gather_fusion.1
  13.1 0.1 select_bitcast_fusion
  13.1 0.1 copy.54
  13.2 0.1 select_n.71
  13.3 0.1 select_n.69
  13.4 35.6 %all_gather.10 = bf16[16,64,192]{2,1,0:T(8,128)(2,1)S(1)} all-gather(bf16[2,64,192]{2,1,0:T(8,128)(2,1)} %param.6), channel_id=1, replica_groups=mesh['ka'=8,'col'=4] {'ka'}, dimensions={0}, use_global_device_ids=true | all-gather | bytes 442368 | tf_op jit(solution)/shard_map/all_gather | solution.py:13
  49.0 0.6 gather_fusion.2
  49.6 0.1 broadcast_select_fusion.1
  49.7 7.1 %all_gather.11 = bf16[4,256,192]{2,1,0:T(8,128)(2,1)S(1)} all-gather(bf16[4,64,192]{2,1,0:T(8,128)(2,1)S(1)} %broadcast_select_fusion.1), channel_id=1, replica_groups=mesh['ka'=8,'col'=4] {'col'}, dimensions={1}, use_global_device_ids=true | all-gather | bytes 491520 | tf_op jit(solution)/shard_map/all_gather | solution.py:15
  56.8 0.0 copy-done
  56.8 0.5 fusion
  57.3 0.1 copy.58
  57.4 33.2 %all-gather.2.cloned.1.call-done = bf16[2,2048,512]{2,1,0:T(8,128)(2,1)} async-done(((bf16[2,256,512]{2,1,0:T(8,128)(2,1)}), bf16[2,2048,512]{2,1,0:T(8,128)(2,1)}) %all-gather.2.cloned.1.call-update) | async-done | bytes 4194320 | tf_op jit(solution)/shard_map/all_gather | solution.py:25
  90.6 6.2 %convolution_convert_fusion = bf16[2,2048,384]{2,1,0:T(8,128)(2,1)} fusion(bf16[2,2048,512]{2,1,0:T(8,128)(2,1)} %all-gather.2.cloned.1.call-done, bf16[2,512,384]{1,2,0:T(8,128)(2,1)S(1)} %bitcast.25), kind=kOutput, calls=%fused_computation.3 | convolution fusion | flops 1612185600 | bytes 8126464 | tf_op jit(solution)/shard_map/qrm,qmx->qrx/dot_general | solution.py:23
  96.8 0.0 copy-start.3
  96.8 0.0 copy-start.1
  96.8 0.0 copy-start.2
  96.8 0.0 reduce-scatter.2.cloned.1.call-update
  96.9 0.0 all-reduce.3.cloned.1.call-start
  96.9 36.5 %reduce-scatter.2.cloned.1.call-done = bf16[2,512,384]{2,1,0:T(8,128)(2,1)} async-done(((bf16[2,2048,384]{2,1,0:T(8,128)(2,1)}), bf16[2,512,384]{2,1,0:T(8,128)(2,1)}) %reduce-scatter.2.cloned.1.call-update) | async-done | bytes 786448 | tf_op jit(solution)/shard_map/reduce_scatter | solution.py:29
  133.4 1.2 convert_reduce_fusion
  134.7 0.2 copy.60
  134.9 0.3 fusion.1
  135.1 0.9 copy.61
  136.0 0.0 all-reduce.3.cloned.1.call-update
  136.0 0.0 copy-done.3
  136.0 0.6 dynamic-slice
  137.3 31.2 %all-reduce.3.cloned.1.call-done = bf16[2,256,192]{2,0,1:T(2,128)(2,1)} async-done(((bf16[2,256,192]{2,0,1:T(2,128)(2,1)}), bf16[2,256,192]{2,0,1:T(2,128)(2,1)}) %all-reduce.3.cloned.1.call-update) | async-done | bytes 196624
  168.5 0.9 constant_dynamic-slice_fusion
  169.4 0.0 copy-done.1
  169.4 0.0 copy-done.2
  169.4 0.7 multiply_add_fusion
  (7 shorter events, 0.0 us)
Async XLA Ops:
  6.5 50.3 %copy-start = (bf16[2,512,256]{2,1,0:T(8,128)(2,1)S(1)}, bf16[2,512,256]{2,1,0:T(8,128)(2,1)}, u32[]{:S(2)}) copy-start(bf16[2,512,256]{2,1,0:T(8,128)(2,1)} %param.7) | copy-start | bytes 1572868
  6.5 84.1 %all-gather.2.cloned.1.call-start = ((), (), s32[]{:S(2)}) async-start(), calls=%async_computation.1 | async-start | bytes 4718592 | tf_op jit(solution)/shard_map/all_gather | solution.py:25
  11.7 121.7 %reduce-scatter.2.cloned.1.call-start = ((), (), s32[]{:S(2)}) async-start(), calls=%async_computation.2 | async-start | bytes 3932160 | tf_op jit(solution)/shard_map/reduce_scatter | solution.py:29
  96.8 39.2 %copy-start.3 = (u32[32]{0:T(128)S(1)}, u32[32]{0:T(128)}, u32[]{:S(2)}) copy-start(u32[32]{0:T(128)} %constant.56) | copy-start | bytes 388
  96.8 72.5 %copy-start.1 = (bf16[2,64,192]{2,1,0:T(8,128)(2,1)S(1)}, bf16[2,64,192]{2,1,0:T(8,128)(2,1)}, u32[]{:S(2)}) copy-start(bf16[2,64,192]{2,1,0:T(8,128)(2,1)} %param.6) | copy-start | bytes 147460
  96.8 72.5 %copy-start.2 = (f32[2,64]{1,0:T(2,128)S(1)}, f32[2,64]{1,0:T(2,128)}, u32[]{:S(2)}) copy-start(f32[2,64]{1,0:T(2,128)} %param.9) | copy-start | bytes 1540
  96.9 71.6 %all-reduce.3.cloned.1.call-start = ((), (), s32[]{:S(2)}) async-start(), calls=%async_computation.3 | async-start | bytes 524288
Sparse Core Ops, SparseCore 0:
  11.8 78.7 all-gather.1
  97.0 36.3 reduce-scatter.1
  136.2 32.2 all-reduce.2
where the time goes:
time: 177 us
  waiting for transfers between devices  101 us (57%)
  blocking collectives  42.7 us (24%)
  between operations  13.9 us (8%)
  local copies, waits for them, and re-layouts  7.5 us (4%)
  matrix products  6.98 us (4%)
  other arithmetic  4.51 us (3%)
    reduce_scatter x1, waiting for transfers between devices, body(): lax.psum_scatter(partials.astype(jnp.bfloat16), 'col', scatter_dimension=...  36.5 us
    all_gather x1, blocking collectives, body(): everyone = lax.all_gather(amps, 'ka', axis=0, tiled=True)  35.6 us
    all_gather x1, waiting for transfers between devices, body(): lax.all_gather(slabs, 'ka', axis=1, tiled=True)  33.2 us
    unnamed x4, waiting for transfers between devices  31.2 us
    all_gather x1, blocking collectives, body(): partners = lax.all_gather(picked, 'col', axis=1, tiled=True)  7.1 us
    dot_general x1, matrix products, body(): jnp.einsum('qrm,qmx->qrx', lax.all_gather(slabs, 'ka', axis=1, tiled=True...  6.23 us
  transfers between devices with their start and end apart: 3, of which 3 were waited for; matrix products, arithmetic and copies ran while one was open for 2% of the time, Pallas kernels for 0%

commit v1 on v0

--- a/solution.py
+++ b/solution.py
@@ -2,6 +2,7 @@
 import jax.numpy as jnp
 from jax import lax
 from jax.sharding import PartitionSpec as P
+from jax.lax import axis_index, axis_size, ppermute
 
 
 def body(amps, isdf_coeffs, w_screen, energies, qsel, partner):
@@ -10,7 +11,20 @@
     offset_base = lax.axis_index("ka") * k_local
     owned = offset_base + jnp.arange(k_local, dtype=jnp.int32)
     wanted = jnp.take(partner, owned, axis=1).reshape(-1)
-    everyone = lax.all_gather(amps, "ka", axis=0, tiled=True)
+
+    def switch_sector(field_in, named_axis):
+        amount_of = axis_size(named_axis)
+        view_out = [(j - 1, j) for j in range(1, amount_of)] + [(amount_of - 1, 0)]
+        earlier = field_in
+        sides = [earlier]
+        for _ in tuple(range(amount_of - 1)):
+            earlier = ppermute(earlier, named_axis, view_out)
+            sides += [earlier]
+        prior = jnp.concatenate([*reversed(sides)], axis=0)
+        even = jnp.roll(prior, (axis_index(named_axis) + 1) * earlier.shape[0], axis=0)
+        return even
+
+    everyone = switch_sector(amps, "ka")
     picked = jnp.take(everyone, wanted, axis=0)
     partners = lax.all_gather(picked, "col", axis=1, tiled=True)
     partners = partners.reshape(2, k_local, partners.shape[1], vectors)

time: 177 us -> 180 us (1.017)
  blocking collectives: 42.7 us -> 7.51 us
  waiting for transfers between devices: 101 us -> 135 us
  starting transfers between devices: 0.09 us -> 3.15 us
    ppermute x0 -> x7, waiting for transfers between devices: none -> 53.6 us  [switch_sector(): earlier = ppermute(earlier, named_axis, view_out)]
    all_gather x1 -> x0, blocking collectives: 35.6 us -> none  [body(): everyone = lax.all_gather(amps, 'ka', axis=0, tiled=True)]
    all_gather x1, waiting for transfers between devices: 33.2 us -> 13.2 us  [body(): lax.all_gather(slabs, 'ka', axis=1, tiled=True)]
    ppermute x0 -> x7, starting transfers between devices: none -> 3.06 us  [switch_sector(): earlier = ppermute(earlier, named_axis, view_out)]
  transfers between devices with their start and end apart: 3 -> 10, of which waited for: 3 -> 10; matrix products, arithmetic and copies ran while one was open for 2% -> 2% of each run, Pallas kernels for 0% -> 0%
where the time goes in v1:
time: 180 us; the launch traced here: 179 us
  waiting for transfers between devices  135 us (75%)
  between operations  14 us (8%)
  local copies, waits for them, and re-layouts  8.51 us (5%)
  blocking collectives  7.51 us (4%)
  matrix products  6.98 us (4%)
  other arithmetic  4.48 us (2%)
  starting transfers between devices  3.15 us (2%)
    ppermute x7, waiting for transfers between devices, switch_sector(): earlier = ppermute(earlier, named_axis, view_out)  53.6 us
    reduce_scatter x1, waiting for transfers between devices, body(): lax.psum_scatter(partials.astype(jnp.bfloat16), 'col', scatter_dimension=...  36.5 us
    unnamed x4, waiting for transfers between devices  31.3 us
    all_gather x1, waiting for transfers between devices, body(): lax.all_gather(slabs, 'ka', axis=1, tiled=True)  13.2 us
    all_gather x1, blocking collectives, body(): partners = lax.all_gather(picked, 'col', axis=1, tiled=True)  7.51 us
    dot_general x1, matrix products, body(): jnp.einsum('qrm,qmx->qrx', lax.all_gather(slabs, 'ka', axis=1, tiled=True...  6.22 us
  transfers between devices with their start and end apart: 10, of which 10 were waited for; matrix products, arithmetic and copies ran while one was open for 2% of the time, Pallas kernels for 0%

profile of v1, /device:TPU:0, one launch (start us, length us, event | category | flops | bytes accessed | tf_op | source)
XLA Modules:
  0.0 179.2 jit_solution(6853676010807923693)
XLA Ops:
  6.6 0.7 compare_select_fusion.4
  7.3 0.7 compare_and_fusion.2
  8.0 0.8 copy.53
  8.7 0.6 gather_fusion.1
  9.3 0.1 select_bitcast_fusion
  9.3 0.1 copy.54
  9.4 0.1 select_n.86
  9.5 2.8 %gather_fusion = bf16[2,256,512]{2,1,0:T(8,128)(2,1)S(1)} fusion(bf16[16,256,512]{2,1,0:T(8,128)(2,1)} %param.8, s32[1024]{0:T(1024)S(1)} %get-tuple-element.6), kind=kCustom, calls=%fused_computation | custom fusion | bytes 1048584 | tf_op jit(solution)/shard_map/jit(_take)/gather | solution.py:36
  12.3 0.9 broadcast_select_fusion
  13.2 0.0 all-gather.2.cloned.1.call-update
  13.3 0.0 reduce-scatter.2.cloned.1.call-start
  13.3 3.0 %collective-permute-start = (bf16[2,64,192]{2,1,0:T(8,128)(2,1)}, bf16[2,64,192]{2,1,0:T(8,128)(2,1)S(1)}, u32[]{:S(2)}, u32[]{:S(2)}) collective-permute-start(bf16[2,64,192]{2,1,0:T(8,128)(2,1)} %param.6), channel_id=1, source_target_pairs={{0,4},{4,8},{8,12},{12,16},{16,20},{20,24},{24,28},{28,0},{1,5},{5... | collective-permute-start | bytes 147464 | tf_op jit(solution)/shard_map/ppermute | solution.py:21
  16.3 5.5 %collective-permute-done = bf16[2,64,192]{2,1,0:T(8,128)(2,1)S(1)} collective-permute-done((bf16[2,64,192]{2,1,0:T(8,128)(2,1)}, bf16[2,64,192]{2,1,0:T(8,128)(2,1)S(1)}, u32[]{:S(2)}, u32[]{:S(2)}) %collective-permute-start) | collective-permute-done | bytes 49184 | tf_op jit(solution)/shard_map/ppermute | solution.py:21
  21.8 0.0 collective-permute-start.1
  21.8 7.1 %collective-permute-done.1 = bf16[2,64,192]{2,1,0:T(8,128)(2,1)S(1)} collective-permute-done((bf16[2,64,192]{2,1,0:T(8,128)(2,1)S(1)}, bf16[2,64,192]{2,1,0:T(8,128)(2,1)S(1)}, u32[]{:S(2)}, u32[]{:S(2)}) %collective-permute-start.1) | collective-permute-done | bytes 49184 | tf_op jit(solution)/shard_map/ppermute | solution.py:21
  28.9 0.0 collective-permute-start.2
  28.9 8.5 %collective-permute-done.2 = bf16[2,64,192]{2,1,0:T(8,128)(2,1)S(1)} collective-permute-done((bf16[2,64,192]{2,1,0:T(8,128)(2,1)S(1)}, bf16[2,64,192]{2,1,0:T(8,128)(2,1)S(1)}, u32[]{:S(2)}, u32[]{:S(2)}) %collective-permute-start.2) | collective-permute-done | bytes 49184 | tf_op jit(solution)/shard_map/ppermute | solution.py:21
  37.4 0.0 collective-permute-start.3
  37.4 8.5 %collective-permute-done.3 = bf16[2,64,192]{2,1,0:T(8,128)(2,1)S(1)} collective-permute-done((bf16[2,64,192]{2,1,0:T(8,128)(2,1)S(1)}, bf16[2,64,192]{2,1,0:T(8,128)(2,1)S(1)}, u32[]{:S(2)}, u32[]{:S(2)}) %collective-permute-start.3) | collective-permute-done | bytes 49184 | tf_op jit(solution)/shard_map/ppermute | solution.py:21
  45.9 0.0 collective-permute-start.4
  45.9 7.0 %collective-permute-done.4 = bf16[2,64,192]{2,1,0:T(8,128)(2,1)S(1)} collective-permute-done((bf16[2,64,192]{2,1,0:T(8,128)(2,1)S(1)}, bf16[2,64,192]{2,1,0:T(8,128)(2,1)S(1)}, u32[]{:S(2)}, u32[]{:S(2)}) %collective-permute-start.4) | collective-permute-done | bytes 49184 | tf_op jit(solution)/shard_map/ppermute | solution.py:21
  52.9 0.0 collective-permute-start.5
  52.9 0.1 select_n.82
  53.0 8.6 %collective-permute-done.5 = bf16[2,64,192]{2,1,0:T(8,128)(2,1)S(1)} collective-permute-done((bf16[2,64,192]{2,1,0:T(8,128)(2,1)S(1)}, bf16[2,64,192]{2,1,0:T(8,128)(2,1)S(1)}, u32[]{:S(2)}, u32[]{:S(2)}) %collective-permute-start.5) | collective-permute-done | bytes 49184 | tf_op jit(solution)/shard_map/ppermute | solution.py:21
  61.6 0.0 collective-permute-start.6
  61.6 8.5 %collective-permute-done.6 = bf16[2,64,192]{2,1,0:T(8,128)(2,1)S(1)} collective-permute-done((bf16[2,64,192]{2,1,0:T(8,128)(2,1)S(1)}, bf16[2,64,192]{2,1,0:T(8,128)(2,1)S(1)}, u32[]{:S(2)}, u32[]{:S(2)}) %collective-permute-start.6) | collective-permute-done | bytes 49184 | tf_op jit(solution)/shard_map/ppermute | solution.py:21
  70.2 0.8 constant_dynamic-update-slice_fusion.8
  71.1 0.0 copy-done.1
  71.2 0.6 gather_fusion.2
  71.8 0.1 broadcast_select_fusion.1
  71.8 7.5 %all_gather.7 = bf16[4,256,192]{2,1,0:T(8,128)(2,1)S(1)} all-gather(bf16[4,64,192]{2,1,0:T(8,128)(2,1)S(1)} %broadcast_select_fusion.1), channel_id=1, replica_groups=mesh['ka'=8,'col'=4] {'col'}, dimensions={1}, use_global_device_ids=true | all-gather | bytes 491520 | tf_op jit(solution)/shard_map/all_gather | solution.py:29
  79.4 0.0 copy-done
  79.4 0.5 fusion
  79.9 0.1 copy.58
  79.9 13.2 %all-gather.2.cloned.1.call-done = bf16[2,2048,512]{2,1,0:T(8,128)(2,1)} async-done(((bf16[2,256,512]{2,1,0:T(8,128)(2,1)}), bf16[2,2048,512]{2,1,0:T(8,128)(2,1)}) %all-gather.2.cloned.1.call-update) | async-done | bytes 4194320 | tf_op jit(solution)/shard_map/all_gather | solution.py:39
  93.1 6.2 %convolution_convert_fusion = bf16[2,2048,384]{2,1,0:T(8,128)(2,1)} fusion(bf16[2,2048,512]{2,1,0:T(8,128)(2,1)} %all-gather.2.cloned.1.call-done, bf16[2,512,384]{1,2,0:T(8,128)(2,1)S(1)} %bitcast.25), kind=kOutput, calls=%fused_computation.3 | convolution fusion | flops 1612185600 | bytes 8126464 | tf_op jit(solution)/shard_map/qrm,qmx->qrx/dot_general | solution.py:37
  99.3 0.0 reduce-scatter.2.cloned.1.call-update
  99.4 0.0 all-reduce.3.cloned.1.call-start
  99.4 36.5 %reduce-scatter.2.cloned.1.call-done = bf16[2,512,384]{2,1,0:T(8,128)(2,1)} async-done(((bf16[2,2048,384]{2,1,0:T(8,128)(2,1)}), bf16[2,512,384]{2,1,0:T(8,128)(2,1)}) %reduce-scatter.2.cloned.1.call-update) | async-done | bytes 786448 | tf_op jit(solution)/shard_map/reduce_scatter | solution.py:43
  135.9 1.2 convert_reduce_fusion
  137.2 0.2 copy.60
  137.4 0.3 fusion.1
  137.7 0.9 copy.61
  138.5 0.0 all-reduce.3.cloned.1.call-update
  138.6 0.6 dynamic-slice
  139.8 31.2 %all-reduce.3.cloned.1.call-done = bf16[2,256,192]{2,0,1:T(2,128)(2,1)} async-done(((bf16[2,256,192]{2,0,1:T(2,128)(2,1)}), bf16[2,256,192]{2,0,1:T(2,128)(2,1)}) %all-reduce.3.cloned.1.call-update) | async-done | bytes 196624
  171.0 0.9 constant_dynamic-slice_fusion
  171.9 0.7 multiply_add_fusion
  (29 shorter events, 0.2 us)
Async XLA Ops:
  6.5 72.8 %copy-start = (bf16[2,512,256]{2,1,0:T(8,128)(2,1)S(1)}, bf16[2,512,256]{2,1,0:T(8,128)(2,1)}, u32[]{:S(2)}) copy-start(bf16[2,512,256]{2,1,0:T(8,128)(2,1)} %param.7) | copy-start | bytes 1572868
  6.5 64.6 %copy-start.1 = (bf16[2,64,192]{2,1,0:T(8,128)(2,1)S(1)}, bf16[2,64,192]{2,1,0:T(8,128)(2,1)}, u32[]{:S(2)}) copy-start(bf16[2,64,192]{2,1,0:T(8,128)(2,1)} %param.6) | copy-start | bytes 147460
  6.5 86.6 %all-gather.2.cloned.1.call-start = ((), (), s32[]{:S(2)}) async-start(), calls=%async_computation.1 | async-start | bytes 4718592 | tf_op jit(solution)/shard_map/all_gather | solution.py:39
  13.3 122.7 %reduce-scatter.2.cloned.1.call-start = ((), (), s32[]{:S(2)}) async-start(), calls=%async_computation.2 | async-start | bytes 3932160 | tf_op jit(solution)/shard_map/reduce_scatter | solution.py:43
  13.3 8.5 %collective-permute-start = (bf16[2,64,192]{2,1,0:T(8,128)(2,1)}, bf16[2,64,192]{2,1,0:T(8,128)(2,1)S(1)}, u32[]{:S(2)}, u32[]{:S(2)}) collective-permute-start(bf16[2,64,192]{2,1,0:T(8,128)(2,1)} %param.6), channel_id=1, source_target_pairs={{0,4},{4,8},{8,12},{12,16},{16,20},{20,24},{24,28},{28,0},{1,5},{5... | collective-permute-start | bytes 147464 | tf_op jit(solution)/shard_map/ppermute | solution.py:21
  21.8 7.1 %collective-permute-start.1 = (bf16[2,64,192]{2,1,0:T(8,128)(2,1)S(1)}, bf16[2,64,192]{2,1,0:T(8,128)(2,1)S(1)}, u32[]{:S(2)}, u32[]{:S(2)}) collective-permute-start(bf16[2,64,192]{2,1,0:T(8,128)(2,1)S(1)} %collective-permute-done), channel_id=1, source_target_pairs={{0,4},{4,8},{8,12},{12,16},{16,20},{20,24},{24,28},{28,0},{1,5},{5... | collective-permute-start | bytes 147464 | tf_op jit(solution)/shard_map/ppermute | solution.py:21
  28.9 8.5 %collective-permute-start.2 = (bf16[2,64,192]{2,1,0:T(8,128)(2,1)S(1)}, bf16[2,64,192]{2,1,0:T(8,128)(2,1)S(1)}, u32[]{:S(2)}, u32[]{:S(2)}) collective-permute-start(bf16[2,64,192]{2,1,0:T(8,128)(2,1)S(1)} %collective-permute-done.1), channel_id=1, source_target_pairs={{0,4},{4,8},{8,12},{12,16},{16,20},{20,24},{24,28},{28,0},{1,5},{5... | collective-permute-start | bytes 147464 | tf_op jit(solution)/shard_map/ppermute | solution.py:21
  37.4 8.5 %collective-permute-start.3 = (bf16[2,64,192]{2,1,0:T(8,128)(2,1)S(1)}, bf16[2,64,192]{2,1,0:T(8,128)(2,1)S(1)}, u32[]{:S(2)}, u32[]{:S(2)}) collective-permute-start(bf16[2,64,192]{2,1,0:T(8,128)(2,1)S(1)} %collective-permute-done.2), channel_id=1, source_target_pairs={{0,4},{4,8},{8,12},{12,16},{16,20},{20,24},{24,28},{28,0},{1,5},{5... | collective-permute-start | bytes 147464 | tf_op jit(solution)/shard_map/ppermute | solution.py:21
  45.9 7.0 %collective-permute-start.4 = (bf16[2,64,192]{2,1,0:T(8,128)(2,1)S(1)}, bf16[2,64,192]{2,1,0:T(8,128)(2,1)S(1)}, u32[]{:S(2)}, u32[]{:S(2)}) collective-permute-start(bf16[2,64,192]{2,1,0:T(8,128)(2,1)S(1)} %collective-permute-done.3), channel_id=1, source_target_pairs={{0,4},{4,8},{8,12},{12,16},{16,20},{20,24},{24,28},{28,0},{1,5},{5... | collective-permute-start | bytes 147464 | tf_op jit(solution)/shard_map/ppermute | solution.py:21
  52.9 8.7 %collective-permute-start.5 = (bf16[2,64,192]{2,1,0:T(8,128)(2,1)S(1)}, bf16[2,64,192]{2,1,0:T(8,128)(2,1)S(1)}, u32[]{:S(2)}, u32[]{:S(2)}) collective-permute-start(bf16[2,64,192]{2,1,0:T(8,128)(2,1)S(1)} %collective-permute-done.4), channel_id=1, source_target_pairs={{0,4},{4,8},{8,12},{12,16},{16,20},{20,24},{24,28},{28,0},{1,5},{5... | collective-permute-start | bytes 147464 | tf_op jit(solution)/shard_map/ppermute | solution.py:21
  61.6 8.5 %collective-permute-start.6 = (bf16[2,64,192]{2,1,0:T(8,128)(2,1)S(1)}, bf16[2,64,192]{2,1,0:T(8,128)(2,1)S(1)}, u32[]{:S(2)}, u32[]{:S(2)}) collective-permute-start(bf16[2,64,192]{2,1,0:T(8,128)(2,1)S(1)} %collective-permute-done.5), channel_id=1, source_target_pairs={{0,4},{4,8},{8,12},{12,16},{16,20},{20,24},{24,28},{28,0},{1,5},{5... | collective-permute-start | bytes 147464 | tf_op jit(solution)/shard_map/ppermute | solution.py:21
  99.3 39.2 %copy-start.3 = (u32[32]{0:T(128)S(1)}, u32[32]{0:T(128)}, u32[]{:S(2)}) copy-start(u32[32]{0:T(128)} %constant.77) | copy-start | bytes 388
  99.3 72.6 %copy-start.2 = (f32[2,64]{1,0:T(2,128)S(1)}, f32[2,64]{1,0:T(2,128)}, u32[]{:S(2)}) copy-start(f32[2,64]{1,0:T(2,128)} %param.9) | copy-start | bytes 1540
  99.4 71.6 %all-reduce.3.cloned.1.call-start = ((), (), s32[]{:S(2)}) async-start(), calls=%async_computation.3 | async-start | bytes 524288
Sparse Core Ops, SparseCore 0:
  13.4 79.6 all-gather.1
  99.5 36.3 reduce-scatter.1
  138.7 32.2 all-reduce.2
